TPU v7x, 32 devices: a whole 2x2x4 slice. The times are simulated.
32 devices in a mesh: ia: 4 (over z), ja: 4 (over x, core), ka: 2 (over y).
Axes of the slice: x: 2, y: 2, z: 4, core: 2. Of those that a mesh axis runs over, the one named last changes fastest.
Arguments:
- tensor: bfloat16 [64, 256, 512], P('ka', 'ia', 'ja'), may hold values from -768 to 768
- observed: int32 [64, 256, 512], P('ka', 'ia', 'ja'), may hold values from 0 to 1, as said below
- factor_a: bfloat16 [256, 128], P('ia', ('ja', 'ka')), may hold values from -6 to 6
- factor_b: bfloat16 [512, 128], P('ja', ('ia', 'ka')), may hold values from -6 to 6
- factor_c: bfloat16 [64, 128], P('ka', ('ia', 'ja')), may hold values from -6 to 6
Outputs:
- step_a: float32 [256, 128], P('ia', ('ja', 'ka'))
- step_b: float32 [512, 128], P('ja', ('ia', 'ka'))
- step_c: float32 [64, 128], P('ka', ('ia', 'ja'))
Inputs may be any that keep to these rules, and one draw needn't show every extreme that they name: `observed`: a 0/1 weight per cell.
All inputs are finite; a program needn't handle non-finite values.
Results may differ from a plain program's by a relative error of at most 0.0095.
Values may be sent and summed in bfloat16 or wider, within the bound.
A program may use at most 64 MiB of HBM per device.

v0:
```python
import jax
import jax.numpy as jnp
from jax import lax
from jax.sharding import PartitionSpec as P

ITERS = 2
DAMP = 1.0


def against(left_side, right_side):
    return lax.dot_general(
        left_side, right_side, (((1,), (1,)), ((), ())), preferred_element_type=jnp.float32
    )


def local(tensor, observed, factor_a, factor_b, factor_c):
    depth_rows, height_rows, width_cols = tensor.shape
    divisor = width_cols * lax.axis_size("ja") * (depth_rows * lax.axis_size("ka")) / 32.0
    full_a = lax.all_gather(factor_a, ("ja", "ka"), axis=1, tiled=True)
    full_b = lax.all_gather(factor_b, ("ia", "ka"), axis=1, tiled=True)
    full_c = lax.all_gather(factor_c, ("ia", "ja"), axis=1, tiled=True)
    columns = full_a.shape[1]
    wide_a = full_a.astype(jnp.float32)
    wide_c = full_c.astype(jnp.float32)
    weight = (observed.astype(jnp.float32) * (1.0 / divisor)).astype(jnp.bfloat16)
    weight = weight.reshape(depth_rows * height_rows, width_cols)
    paired = (
        (wide_c[:, None, :] * wide_a[None, :, :])
        .astype(jnp.bfloat16)
        .reshape(depth_rows * height_rows, columns)
    )

    def partials(weighted):
        part_b = lax.dot_general(
            weighted, paired, (((0,), (0,)), ((), ())), preferred_element_type=jnp.float32
        )
        mixture = jnp.dot(weighted, full_b, preferred_element_type=jnp.float32).reshape(
            depth_rows, height_rows, columns
        )
        part_a = jnp.einsum("kir,kr->ir", mixture, wide_c)
        part_c = jnp.einsum("kir,ir->kr", mixture, wide_a)
        return (part_a, part_b, part_c)

    def settle(parts):
        total_a = lax.psum(parts[0], ("ja", "ka"))
        total_b = lax.psum(parts[1], ("ia", "ka"))
        total_c = lax.psum(parts[2], ("ia", "ja"))
        return (total_a, total_b, total_c)

    scales = (
        1.0 / lax.axis_size(("ja", "ka")),
        1.0 / lax.axis_size(("ia", "ka")),
        1.0 / lax.axis_size(("ia", "ja")),
    )

    def inner_sum(first, second):
        local_sum = sum(
            (
                jnp.sum(left_side * right_side) * factor
                for left_side, right_side, factor in zip(first, second, scales)
            )
        )
        return lax.psum(local_sum, ("ia", "ja", "ka"))

    def expand(direction):
        hat_a = direction[0].astype(jnp.bfloat16)
        hat_b = direction[1].astype(jnp.bfloat16)
        hat_c = direction[2].astype(jnp.bfloat16)
        return (hat_a, hat_b, hat_c)

    def hessian_times(direction):
        hat_a, hat_b, hat_c = expand(direction)
        sideways = (
            hat_c.astype(jnp.float32)[:, None, :] * wide_a[None, :, :]
            + wide_c[:, None, :] * hat_a.astype(jnp.float32)[None, :, :]
        )
        sideways = sideways.astype(jnp.bfloat16).reshape(depth_rows * height_rows, columns)
        tangent = against(paired, hat_b) + against(sideways, full_b)
        weighted = (weight.astype(jnp.float32) * tangent).astype(jnp.bfloat16)
        parts = settle(partials(weighted))
        return tuple((part + DAMP * vector for part, vector in zip(parts, direction)))

    fitted = against(paired, full_b)
    values = tensor.reshape(depth_rows * height_rows, width_cols).astype(jnp.float32)
    errors = (weight.astype(jnp.float32) * (values - fitted)).astype(jnp.bfloat16)
    gradient = settle(partials(errors))
    solution = tuple((jnp.zeros_like(vector) for vector in gradient))
    residual = gradient
    direction = gradient
    norm_now = inner_sum(residual, residual)
    for iteration in range(ITERS):
        product = hessian_times(direction)
        step_size = norm_now / inner_sum(direction, product)
        solution = tuple(
            (vector + step_size * update for vector, update in zip(solution, direction))
        )
        if iteration + 1 < ITERS:
            residual = tuple(
                (vector - step_size * update for vector, update in zip(residual, product))
            )
            norm_next = inner_sum(residual, residual)
            direction = tuple(
                (
                    vector + norm_next / norm_now * update
                    for vector, update in zip(residual, direction)
                )
            )
            norm_now = norm_next
    position_a = lax.axis_index(("ja", "ka")) * factor_a.shape[1]
    position_b = lax.axis_index(("ia", "ka")) * factor_b.shape[1]
    position_c = lax.axis_index(("ia", "ja")) * factor_c.shape[1]
    step_a = lax.dynamic_slice_in_dim(solution[0], position_a, factor_a.shape[1], 1)
    step_b = lax.dynamic_slice_in_dim(solution[1], position_b, factor_b.shape[1], 1)
    step_c = lax.dynamic_slice_in_dim(solution[2], position_c, factor_c.shape[1], 1)
    return (step_a, step_b, step_c)


def solution(mesh):
    placed = (
        P("ka", "ia", "ja"),
        P("ka", "ia", "ja"),
        P("ia", ("ja", "ka")),
        P("ja", ("ia", "ka")),
        P("ka", ("ia", "ja")),
    )
    return jax.shard_map(
        local,
        mesh=mesh,
        in_specs=placed,
        out_specs=(P("ia", ("ja", "ka")), P("ja", ("ia", "ka")), P("ka", ("ia", "ja"))),
        check_vma=False,
    )
```

profile of v0, /device:TPU:0, one launch (start us, length us, event | category | flops | bytes accessed | tf_op | source)
XLA Modules:
  0.0 519.4 jit_solution(12304898515846047202)
XLA Ops:
  7.2 14.5 %all_gather.10 = bf16[64,128]{0,1:T(8,128)(2,1)S(1)} all-gather(bf16[64,16]{0,1:T(8,128)(2,1)} %param.7), channel_id=1, replica_groups=mesh['ia'=4,'ja'=4,'ka'=2] {'ja','ka'}, dimensions={1}, use_global_device_ids=true | all-gather | bytes 18432 | tf_op jit(solution)/shard_map/all_gather | solution.py:19
  21.8 0.7 copy-done.3
  22.4 21.9 %all_gather.9 = bf16[32,128]{0,1:T(8,128)(2,1)S(1)} all-gather(bf16[32,8]{0,1:T(8,128)(2,1)S(1)} %copy-done.3), channel_id=1, replica_groups=mesh['ia'=4,'ja'=4,'ka'=2] {'ia','ja'}, dimensions={1}, use_global_device_ids=true | all-gather | bytes 8704 | tf_op jit(solution)/shard_map/all_gather | solution.py:21
  44.4 0.7 copy-done.2
  45.1 30.6 %all_gather.11 = bf16[128,128]{0,1:T(8,128)(2,1)S(1)} all-gather(bf16[128,16]{0,1:T(8,128)(2,1)S(1)} %copy-done.2), channel_id=1, replica_groups=mesh['ia'=4,'ja'=4,'ka'=2] {'ia','ka'}, dimensions={1}, use_global_device_ids=true | all-gather | bytes 36864 | tf_op jit(solution)/shard_map/all_gather | solution.py:20
  75.7 1.4 multiply_convert_fusion.1
  77.2 0.9 copy-done.1
  78.4 1.0 fusion.16
  80.1 22.7 %psum.91 = f32[64,128]{1,0:T(8,128)S(1)} all-reduce(f32[64,128]{1,0:T(8,128)S(1)} %bitcast.75), channel_id=1, replica_groups=mesh['ia'=4,'ja'=4,'ka'=2] {'ja','ka'}, use_global_device_ids=true, to_apply=%region_0.0 | all-reduce | flops 8192 | bytes 65536 | tf_op jit(solution)/shard_map/psum | solution.py:45
  102.8 58.1 %psum.93 = f32[32,128]{1,0:T(8,128)S(1)} all-reduce(f32[32,128]{1,0:T(8,128)S(1)} %bitcast.78), channel_id=1, replica_groups=mesh['ia'=4,'ja'=4,'ka'=2] {'ia','ja'}, use_global_device_ids=true, to_apply=%region_4.0 | all-reduce | flops 4096 | bytes 32768 | tf_op jit(solution)/shard_map/psum | solution.py:47
  161.0 1.1 fusion.12
  162.5 1.0 fusion.17
  164.0 23.9 %psum.95 = f32[64,128]{1,0:T(8,128)S(1)} all-reduce(f32[64,128]{1,0:T(8,128)S(1)} %bitcast.76), channel_id=1, replica_groups=mesh['ia'=4,'ja'=4,'ka'=2] {'ja','ka'}, use_global_device_ids=true, to_apply=%region_7.0 | all-reduce | flops 8192 | bytes 65536 | tf_op jit(solution)/shard_map/psum | solution.py:45
  187.8 0.6 multiply_reduce_fusion.10
  188.4 57.7 %psum.97 = f32[32,128]{1,0:T(8,128)S(1)} all-reduce(f32[32,128]{1,0:T(8,128)S(1)} %bitcast.77), channel_id=1, replica_groups=mesh['ia'=4,'ja'=4,'ka'=2] {'ia','ja'}, use_global_device_ids=true, to_apply=%region_11.0 | all-reduce | flops 4096 | bytes 32768 | tf_op jit(solution)/shard_map/psum | solution.py:47
  246.2 0.7 multiply_reduce_fusion.13
  248.1 1.5 multiply_reduce_fusion.7
  252.3 36.9 %all-reduce = (f32[]{:T(128)}, f32[]{:T(128)}) all-reduce(f32[]{:T(128)S(6)} %add.125, f32[]{:T(128)S(6)} %add.132), channel_id=1, replica_groups=mesh['ia'=4,'ja'=4,'ka'=2] {'ia','ja','ka'}, use_global_device_ids=true, to_apply=%region_6.0 | all-reduce | flops 2 | bytes 16 | tf_op jit(solution)/shard_map/psum | solution.py:63
  290.5 0.6 multiply_reduce_fusion.12
  291.8 0.6 multiply_reduce_fusion.9
  292.4 0.6 multiply_reduce_fusion.6
  294.3 41.9 %psum.99 = f32[]{:T(128)} all-reduce(f32[]{:T(128)S(6)} %add.134), channel_id=1, replica_groups=mesh['ia'=4,'ja'=4,'ka'=2] {'ia','ja','ka'}, use_global_device_ids=true, to_apply=%region_17.0 | all-reduce | flops 1 | bytes 8 | tf_op jit(solution)/shard_map/psum | solution.py:63
  338.7 1.0 fusion.18
  339.6 59.3 %psum.102 = f32[32,128]{1,0:T(8,128)S(1)} all-reduce(f32[32,128]{1,0:T(8,128)S(1)} %bitcast.79), channel_id=1, replica_groups=mesh['ia'=4,'ja'=4,'ka'=2] {'ia','ja'}, use_global_device_ids=true, to_apply=%region_22.0 | all-reduce | flops 4096 | bytes 32768 | tf_op jit(solution)/shard_map/psum | solution.py:47
  400.3 23.2 %psum.100 = f32[64,128]{1,0:T(8,128)S(1)} all-reduce(f32[64,128]{1,0:T(8,128)S(1)} %bitcast.74), channel_id=1, replica_groups=mesh['ia'=4,'ja'=4,'ka'=2] {'ja','ka'}, use_global_device_ids=true, to_apply=%region_18.0 | all-reduce | flops 8192 | bytes 65536 | tf_op jit(solution)/shard_map/psum | solution.py:45
  423.5 0.6 fusion.8
  424.1 42.1 %all-reduce.9.cloned.1.call-done = f32[128,128]{1,0:T(8,128)} async-done(((f32[128,128]{1,0:T(8,128)}), f32[128,128]{1,0:T(8,128)}) %all-reduce.9.cloned.1.call-update) | async-done | bytes 65552 | tf_op jit(solution)/shard_map/psum | solution.py:46
  466.2 1.5 fusion.6
  469.0 40.3 %psum.103 = f32[]{:T(128)} all-reduce(f32[]{:T(128)S(6)} %add.144), channel_id=1, replica_groups=mesh['ia'=4,'ja'=4,'ka'=2] {'ia','ja','ka'}, use_global_device_ids=true, to_apply=%region_24.0 | all-reduce | flops 1 | bytes 8 | tf_op jit(solution)/shard_map/psum | solution.py:63
  510.7 0.7 copy.24
  511.5 0.7 copy.23
  512.2 0.7 copy.22
  (43 shorter events, 4.4 us)
Async XLA Ops:
  7.2 153.9 %all-reduce.5.cloned.1.call-start = ((), (), s32[]{:S(2)}) async-start(), calls=%async_computation | async-start | bytes 131072 | tf_op jit(solution)/shard_map/psum | solution.py:46
  21.8 0.7 copy-start.3
  44.4 0.7 copy-start.2
  77.0 1.0 copy-start.1
  79.4 168.7 %all-reduce.7.cloned.1.call-start = ((), (), s32[]{:S(2)}) async-start(), calls=%async_computation.1 | async-start | bytes 131072 | tf_op jit(solution)/shard_map/psum | solution.py:46
  163.8 302.5 %all-reduce.9.cloned.1.call-start = ((), (), s32[]{:S(2)}) async-start(), calls=%async_computation.2 | async-start | bytes 131072 | tf_op jit(solution)/shard_map/psum | solution.py:46
  188.4 59.7 %copy-start = (f32[128,128]{1,0:T(8,128)S(1)}, f32[128,128]{1,0:T(8,128)}, u32[]{:S(2)}) copy-start(f32[128,128]{1,0:T(8,128)} %all-reduce.5.cloned.1.call-done) | copy-start | bytes 196612
Sparse Core Ops, SparseCore 0:
  79.5 66.1 all-reduce.4
  163.9 66.5 all-reduce.6
  400.3 65.8 all-reduce.8
where the time goes:
time: 520 us; the launch traced here: 519 us
  blocking collectives  431 us (83%)
  waiting for transfers between devices  42.2 us (8%)
  between operations  25.8 us (5%)
  other arithmetic  9.88 us (2%)
  matrix products  6.15 us (1%)
    psum x3, blocking collectives, settle(): total_c = lax.psum(parts[2], ('ia', 'ja'))  175 us
    psum x3, blocking collectives, inner_sum(): return lax.psum(local_sum, ('ia', 'ja', 'ka'))  119 us
    psum x3, blocking collectives, settle(): total_a = lax.psum(parts[0], ('ja', 'ka'))  69.7 us
    psum x3, waiting for transfers between devices, settle(): total_b = lax.psum(parts[1], ('ia', 'ka'))  42.1 us
    all_gather x1, blocking collectives, local(): full_b = lax.all_gather(factor_b, ('ia', 'ka'), axis=1, tiled=True)  30.6 us
    all_gather x1, blocking collectives, local(): full_c = lax.all_gather(factor_c, ('ia', 'ja'), axis=1, tiled=True)  21.9 us
    all_gather x1, blocking collectives, local(): full_a = lax.all_gather(factor_a, ('ja', 'ka'), axis=1, tiled=True)  14.5 us
  transfers between devices with their start and end apart: 3, of which 1 were waited for; matrix products, arithmetic and copies ran while one was open for 1% of the time, Pallas kernels for 0%

commit v1 on v0

--- a/solution.py
+++ b/solution.py
@@ -60,7 +60,11 @@
                 for left_side, right_side, factor in zip(first, second, scales)
             )
         )
-        return lax.psum(local_sum, ("ia", "ja", "ka"))
+
+        def meet_slabs_in(axis_id, ax_name, raw):
+            return lax.psum(lax.psum(raw, axis_id), ax_name)
+
+        return meet_slabs_in("ia", ("ja", "ka"), local_sum)
 
     def expand(direction):
         hat_a = direction[0].astype(jnp.bfloat16)

time: 520 us -> 472 us (0.908)
  blocking collectives: 431 us -> 382 us
    psum x3 -> x6, blocking collectives: 119 us -> 72.3 us  [meet_slabs_in(): return lax.psum(lax.psum(raw, axis_id), ax_name)]
where the time goes in v1:
time: 472 us; the launch traced here: 471 us
  blocking collectives  382 us (81%)
  waiting for transfers between devices  42.2 us (9%)
  between operations  25.8 us (5%)
  other arithmetic  9.88 us (2%)
  matrix products  6.16 us (1%)
    psum x3, blocking collectives, settle(): total_c = lax.psum(parts[2], ('ia', 'ja'))  173 us
    psum x6, blocking collectives, meet_slabs_in(): return lax.psum(lax.psum(raw, axis_id), ax_name)  72.3 us
    psum x3, blocking collectives, settle(): total_a = lax.psum(parts[0], ('ja', 'ka'))  69.7 us
    psum x3, waiting for transfers between devices, settle(): total_b = lax.psum(parts[1], ('ia', 'ka'))  42.1 us
    all_gather x1, blocking collectives, local(): full_b = lax.all_gather(factor_b, ('ia', 'ka'), axis=1, tiled=True)  30.6 us
    all_gather x1, blocking collectives, local(): full_c = lax.all_gather(factor_c, ('ia', 'ja'), axis=1, tiled=True)  21.9 us
    all_gather x1, blocking collectives, local(): full_a = lax.all_gather(factor_a, ('ja', 'ka'), axis=1, tiled=True)  14.5 us
  transfers between devices with their start and end apart: 3, of which 1 were waited for; matrix products, arithmetic and copies ran while one was open for 1% of the time, Pallas kernels for 0%

profile of v1, /device:TPU:0, one launch (start us, length us, event | category | flops | bytes accessed | tf_op | source)
XLA Modules:
  0.0 471.0 jit_solution(3898853795339588339)
XLA Ops:
  7.2 14.5 %all_gather.10 = bf16[64,128]{0,1:T(8,128)(2,1)S(1)} all-gather(bf16[64,16]{0,1:T(8,128)(2,1)} %param.7), channel_id=1, replica_groups=mesh['ia'=4,'ja'=4,'ka'=2] {'ja','ka'}, dimensions={1}, use_global_device_ids=true | all-gather | bytes 18432 | tf_op jit(solution)/shard_map/all_gather | solution.py:19
  21.8 0.7 copy-done.3
  22.4 21.9 %all_gather.9 = bf16[32,128]{0,1:T(8,128)(2,1)S(1)} all-gather(bf16[32,8]{0,1:T(8,128)(2,1)S(1)} %copy-done.3), channel_id=1, replica_groups=mesh['ia'=4,'ja'=4,'ka'=2] {'ia','ja'}, dimensions={1}, use_global_device_ids=true | all-gather | bytes 8704 | tf_op jit(solution)/shard_map/all_gather | solution.py:21
  44.4 0.7 copy-done.2
  45.1 30.6 %all_gather.11 = bf16[128,128]{0,1:T(8,128)(2,1)S(1)} all-gather(bf16[128,16]{0,1:T(8,128)(2,1)S(1)} %copy-done.2), channel_id=1, replica_groups=mesh['ia'=4,'ja'=4,'ka'=2] {'ia','ka'}, dimensions={1}, use_global_device_ids=true | all-gather | bytes 36864 | tf_op jit(solution)/shard_map/all_gather | solution.py:20
  75.7 1.4 multiply_convert_fusion.1
  77.2 0.9 copy-done.1
  78.4 1.0 fusion.16
  80.1 22.7 %psum.119 = f32[64,128]{1,0:T(8,128)S(1)} all-reduce(f32[64,128]{1,0:T(8,128)S(1)} %bitcast.75), channel_id=1, replica_groups=mesh['ia'=4,'ja'=4,'ka'=2] {'ja','ka'}, use_global_device_ids=true, to_apply=%region_0.0 | all-reduce | flops 8192 | bytes 65536 | tf_op jit(solution)/shard_map/psum | solution.py:45
  102.8 58.1 %psum.121 = f32[32,128]{1,0:T(8,128)S(1)} all-reduce(f32[32,128]{1,0:T(8,128)S(1)} %bitcast.78), channel_id=1, replica_groups=mesh['ia'=4,'ja'=4,'ka'=2] {'ia','ja'}, use_global_device_ids=true, to_apply=%region_4.0 | all-reduce | flops 4096 | bytes 32768 | tf_op jit(solution)/shard_map/psum | solution.py:47
  161.0 1.1 fusion.12
  162.5 1.0 fusion.17
  164.0 23.9 %psum.124 = f32[64,128]{1,0:T(8,128)S(1)} all-reduce(f32[64,128]{1,0:T(8,128)S(1)} %bitcast.76), channel_id=1, replica_groups=mesh['ia'=4,'ja'=4,'ka'=2] {'ja','ka'}, use_global_device_ids=true, to_apply=%region_8.0 | all-reduce | flops 8192 | bytes 65536 | tf_op jit(solution)/shard_map/psum | solution.py:45
  187.8 0.6 multiply_reduce_fusion.10
  188.4 57.7 %psum.126 = f32[32,128]{1,0:T(8,128)S(1)} all-reduce(f32[32,128]{1,0:T(8,128)S(1)} %bitcast.77), channel_id=1, replica_groups=mesh['ia'=4,'ja'=4,'ka'=2] {'ia','ja'}, use_global_device_ids=true, to_apply=%region_12.0 | all-reduce | flops 4096 | bytes 32768 | tf_op jit(solution)/shard_map/psum | solution.py:47
  246.2 0.7 multiply_reduce_fusion.13
  248.1 1.5 multiply_reduce_fusion.7
  252.3 8.9 %all-reduce.1 = (f32[]{:T(128)}, f32[]{:T(128)}) all-reduce(f32[]{:T(128)S(6)} %add.133, f32[]{:T(128)S(6)} %add.140), channel_id=1, replica_groups=mesh['ia'=4,'ja'=4,'ka'=2] {'ia'}, use_global_device_ids=true, to_apply=%region_6.0 | all-reduce | flops 2 | bytes 16 | tf_op jit(solution)/shard_map/psum | solution.py:65
  261.2 13.4 %all-reduce = (f32[]{:T(128)}, f32[]{:T(128)}) all-reduce(f32[]{:T(128)} %get-tuple-element.20, f32[]{:T(128)} %get-tuple-element.21), channel_id=1, replica_groups=mesh['ia'=4,'ja'=4,'ka'=2] {'ja','ka'}, use_global_device_ids=true, to_apply=%region_7.0 | all-reduce | flops 2 | bytes 16 | tf_op jit(solution)/shard_map/psum | solution.py:65
  277.8 0.6 multiply_reduce_fusion.6
  279.7 10.9 %psum.129 = f32[]{:T(128)} all-reduce(f32[]{:T(128)S(6)} %add.142), channel_id=1, replica_groups=mesh['ia'=4,'ja'=4,'ka'=2] {'ia'}, use_global_device_ids=true, to_apply=%region_19.0 | all-reduce | flops 1 | bytes 8 | tf_op jit(solution)/shard_map/psum | solution.py:65
  290.6 13.9 %psum.130 = f32[]{:T(128)} all-reduce(f32[]{:T(128)} %psum.129), channel_id=1, replica_groups=mesh['ia'=4,'ja'=4,'ka'=2] {'ja','ka'}, use_global_device_ids=true, to_apply=%region_20.0 | all-reduce | flops 1 | bytes 8 | tf_op jit(solution)/shard_map/psum | solution.py:65
  306.9 1.0 fusion.18
  307.9 57.6 %psum.133 = f32[32,128]{1,0:T(8,128)S(1)} all-reduce(f32[32,128]{1,0:T(8,128)S(1)} %bitcast.79), channel_id=1, replica_groups=mesh['ia'=4,'ja'=4,'ka'=2] {'ia','ja'}, use_global_device_ids=true, to_apply=%region_25.0 | all-reduce | flops 4096 | bytes 32768 | tf_op jit(solution)/shard_map/psum | solution.py:47
  366.9 23.2 %psum.131 = f32[64,128]{1,0:T(8,128)S(1)} all-reduce(f32[64,128]{1,0:T(8,128)S(1)} %bitcast.74), channel_id=1, replica_groups=mesh['ia'=4,'ja'=4,'ka'=2] {'ja','ka'}, use_global_device_ids=true, to_apply=%region_21.0 | all-reduce | flops 8192 | bytes 65536 | tf_op jit(solution)/shard_map/psum | solution.py:45
  390.8 42.1 %all-reduce.10.cloned.1.call-done = f32[128,128]{1,0:T(8,128)} async-done(((f32[128,128]{1,0:T(8,128)}), f32[128,128]{1,0:T(8,128)}) %all-reduce.10.cloned.1.call-update) | async-done | bytes 65552 | tf_op jit(solution)/shard_map/psum | solution.py:46
  432.9 1.5 fusion.6
  435.6 11.2 %psum.134 = f32[]{:T(128)} all-reduce(f32[]{:T(128)S(6)} %add.152), channel_id=1, replica_groups=mesh['ia'=4,'ja'=4,'ka'=2] {'ia'}, use_global_device_ids=true, to_apply=%region_27.0 | all-reduce | flops 1 | bytes 8 | tf_op jit(solution)/shard_map/psum | solution.py:65
  446.9 14.0 %psum.135 = f32[]{:T(128)} all-reduce(f32[]{:T(128)} %psum.134), channel_id=1, replica_groups=mesh['ia'=4,'ja'=4,'ka'=2] {'ja','ka'}, use_global_device_ids=true, to_apply=%region_28.0 | all-reduce | flops 1 | bytes 8 | tf_op jit(solution)/shard_map/psum | solution.py:65
  462.3 0.7 copy.24
  463.1 0.7 copy.23
  463.8 0.7 copy.22
  (46 shorter events, 6.3 us)
Async XLA Ops:
  7.2 153.9 %all-reduce.6.cloned.1.call-start = ((), (), s32[]{:S(2)}) async-start(), calls=%async_computation | async-start | bytes 131072 | tf_op jit(solution)/shard_map/psum | solution.py:46
  21.8 0.7 copy-start.3
  44.4 0.7 copy-start.2
  77.0 1.0 copy-start.1
  79.4 168.7 %all-reduce.8.cloned.1.call-start = ((), (), s32[]{:S(2)}) async-start(), calls=%async_computation.1 | async-start | bytes 131072 | tf_op jit(solution)/shard_map/psum | solution.py:46
  163.8 269.1 %all-reduce.10.cloned.1.call-start = ((), (), s32[]{:S(2)}) async-start(), calls=%async_computation.2 | async-start | bytes 131072 | tf_op jit(solution)/shard_map/psum | solution.py:46
  188.4 59.7 %copy-start = (f32[128,128]{1,0:T(8,128)S(1)}, f32[128,128]{1,0:T(8,128)}, u32[]{:S(2)}) copy-start(f32[128,128]{1,0:T(8,128)} %all-reduce.6.cloned.1.call-done) | copy-start | bytes 196612
Sparse Core Ops, SparseCore 0:
  79.5 66.1 all-reduce.5
  163.9 66.5 all-reduce.7
  366.9 65.9 all-reduce.9
